TPU v7x, 32 devices: a whole 2x2x4 slice. The times are simulated.
32 devices in a mesh: region: 16 (over z, y, x), mp: 2 (over core).
Axes of the slice: x: 2, y: 2, z: 4, core: 2. Of those that a mesh axis runs over, the one named last changes fastest.
Arguments:
- tokens: bfloat16 [16384, 1024], P('region')
- ln_gain: bfloat16 [1024], replicated, may hold values from 0.25 to 1.75
- w_qkv: bfloat16 [1024, 3, 1024], P(None, None, 'mp')
- w_out: bfloat16 [1024, 1024], P('mp'), may hold values from -0.75 to 0.75
- neighbours: int32 [256, 8], P('region'), may hold values from 0 to 255, as said below
- degree: int32 [256], P('region'), may hold values from 1 to 8
Outputs:
- update: bfloat16 [16384, 1024], P('region')
Inputs may be any that keep to these rules, and one draw needn't show every extreme that they name: A neighbour of a patch with local index below 2 in its region (local index = id % 16, region = id // 16) lies in the same region or is one of the last 2 patches of region r-1 or r-2 (cyclically); of local index 14 or more: same region or one of the first 2 patches of region r+1 or r+2; any other patch's neighbours lie in its own region. Only the first degree[p] entries of a row count.
All inputs are finite; a program needn't handle non-finite values.
Results may differ from a plain program's by a relative error of at most 0.012.
The roundings to bfloat16 on the way count: a program that leaves them out, or rounds other values in their place, can miss the bound.
Values may be sent and summed in bfloat16 or wider, within the bound.
A program may use at most 192 MiB of HBM per device.

v0:
```python
import jax
import jax.numpy as jnp
from jax import lax
from jax.sharding import PartitionSpec as P

HDIM = 64
NBR = 8
RIM = 2


def spread_2(value, axis, source):
    kept = jnp.where(lax.axis_index(axis) == source, value, 0).astype(value.dtype)
    return lax.psum(kept, axis)


def from_behind(block, axis, distance):
    devices = range(lax.axis_size(axis))
    route = [((i - distance) % len(devices), i) for i in devices]
    return lax.ppermute(block, axis, route)


def layer_norm(rows, gain):
    values = rows.astype(jnp.float32)
    centre = jnp.mean(values, axis=-1, keepdims=True)
    spread = jnp.mean((values - centre) ** 2, axis=-1, keepdims=True)
    return ((values - centre) * lax.rsqrt(spread + 1e-05) * gain.astype(jnp.float32)).astype(
        jnp.bfloat16
    )


def project(block, w_flat, feat):
    out = jnp.dot(block, w_flat, preferred_element_type=jnp.float32).reshape(-1, 3, feat)
    query = (out[:, 0, :] * (1.0 / HDIM**0.5)).astype(jnp.bfloat16)
    pair = jnp.stack([out[:, 1, :].astype(jnp.bfloat16), out[:, 2, :].astype(jnp.bfloat16)], axis=1)
    return (query, pair)


def attend_block(query, pairs, valid, heads):
    npat, keys = (pairs.shape[0], pairs.shape[1])
    patch = query.shape[1]
    query = query.reshape(npat, patch, heads, HDIM)
    key_part = pairs[:, :, 0, :].reshape(npat, keys, heads, HDIM)
    value_part = pairs[:, :, 1, :].reshape(npat, keys, heads, HDIM)
    scores = jnp.einsum("pqhd,pkhd->phqk", query, key_part, preferred_element_type=jnp.float32)
    scores = jnp.where(valid[:, None, None, :], scores, jnp.float32(-1e30))
    top = jnp.max(scores, axis=-1, keepdims=True)
    expo = jnp.exp(scores - top)
    total = jnp.sum(expo, axis=-1)
    weights = expo.astype(jnp.bfloat16)
    context = jnp.einsum("phqk,pkhd->pqhd", weights, value_part, preferred_element_type=jnp.float32)
    context = context / jnp.transpose(total, (0, 2, 1))[..., None]
    return context.astype(jnp.bfloat16).reshape(npat * patch, heads * HDIM)


def per_device(tokens, ln_gain, w_qkv, w_out, neighbours, degree):
    rows, width = tokens.shape
    npat = neighbours.shape[0]
    patch = rows // npat
    feat = w_qkv.shape[2]
    heads_here = feat // HDIM
    rim = RIM
    normed = layer_norm(tokens, ln_gain)
    w_flat = w_qkv.reshape(width, 3 * feat)
    query, pairs = project(normed, w_flat, feat)
    kv_pat = pairs.reshape(npat, patch, 2, feat)
    anchor = spread_2(kv_pat[0], "region", 0)

    def fetch_before(step):
        return from_behind(kv_pat[npat - rim :], "region", step)

    def fetch_after(step):
        return from_behind(kv_pat[:rim], "region", step)

    table = jnp.concatenate(
        [kv_pat, fetch_before(1), fetch_before(2), fetch_after(-1), fetch_after(-2)], axis=0
    )
    cycle = lax.axis_size("region")
    region_id = lax.axis_index("region")
    owner = neighbours // npat
    local = neighbours % npat
    reach = (owner - region_id) % cycle
    slot = jnp.where(
        reach == 0,
        local,
        jnp.where(
            reach == cycle - 1,
            npat + local - (npat - rim),
            jnp.where(
                reach == cycle - 2,
                npat + rim + local - (npat - rim),
                jnp.where(reach == 1, npat + 2 * rim + local, npat + 3 * rim + local),
            ),
        ),
    )
    far = table[slot].reshape(npat, NBR * patch, 2, feat)
    anchors = jnp.broadcast_to(anchor[None], (npat, patch, 2, feat))
    keyed = jnp.concatenate([kv_pat, far, anchors], axis=1)
    slot_ok = jnp.arange(NBR, dtype=jnp.int32)[None, :] < degree[:, None]
    far_ok = jnp.repeat(slot_ok, patch, axis=1)
    ones = jnp.ones((npat, patch), dtype=bool)
    valid = jnp.concatenate([ones, far_ok, ones], axis=1)
    context = attend_block(query.reshape(npat, patch, feat), keyed, valid, heads_here)
    partial_sum = jnp.dot(context, w_out, preferred_element_type=jnp.float32)
    return lax.psum(partial_sum, "mp").astype(jnp.bfloat16)


def solution(mesh):
    placed = (
        P("region", None),
        P(),
        P(None, None, "mp"),
        P("mp", None),
        P("region", None),
        P("region"),
    )
    return jax.shard_map(
        per_device, mesh=mesh, in_specs=placed, out_specs=P("region", None), check_vma=False
    )
```

profile of v0, /device:TPU:11, one launch (start us, length us, event | category | flops | bytes accessed | tf_op | source)
XLA Modules:
  0.0 279.4 jit_solution(11935173775363583606)
XLA Ops:
  6.5 0.8 convert_element_type.32
  7.3 1.9 convert_reduce_fusion
  9.3 0.0 copy-start.3
  9.3 2.4 fusion.9
  11.7 4.7 %copy.11 = bf16[1024,3,512]{0,2,1:T(8,128)(2,1)} copy(bf16[1024,3,512]{2,0,1:T(8,128)(2,1)} %param.8) | data formatting | bytes 6291456 | tf_op args[2]
  16.4 7.5 %fusion.32 = (bf16[1024,3,512]{2,0,1:T(8,128)(2,1)S(1)}, f32[1024,3,512]{2,0,1:T(8,128)}) fusion(bf16[1024,3,512]{0,2,1:T(8,128)(2,1)} %copy.11, bf16[1024,1024]{1,0:T(8,128)(2,1)S(1)} %copy-done.3, f32[1024]{0:T(1024)S(1)} %convert_element_type.32, f32[1024]{0:T(1024)S(1)} %add_rsqrt_fusion, f32[1024]{0:T(1024)S(1)} %broadcast_multiply_fusion), kind=kOutput, calls=%fused_computation.57 | convolution fusion | flops 3228041216 | bytes 14692352 | tf_op jit(solution)/shard_map/dot_general | solution.py:32
  23.9 1.7 copy-done.4
  25.6 0.9 fusion.30
  26.5 1.2 collective-permute-start.1
  27.7 1.2 collective-permute-start
  28.9 1.1 collective-permute-start.3
  30.1 0.3 collective-permute-start.2
  30.3 1.6 slice_select_fusion
  31.9 0.0 all-reduce.3.cloned.1.call-update
  31.9 1.7 fusion.31
  33.6 0.1 iota_compare_fusion
  33.7 3.5 %fusion.19 = bf16[1024,1,512]{2,0,1:T(8,128)(2,1)} fusion(f32[1024,3,512]{2,0,1:T(8,128)} %get-tuple-element.12), kind=kLoop, calls=%fused_computation.23 | loop fusion | flops 1048576 | bytes 3145728 | tf_op jit(solution)/shard_map/convert_element_type | solution.py:33
  37.2 0.0 copy-done.1
  37.2 1.5 maximum_dynamic-update-slice_fusion
  38.7 0.1 broadcast_in_dim.43
  38.8 0.1 reshape.45
  38.9 0.1 pad_add_fusion
  39.0 0.1 copy.12
  39.1 0.1 reshape.49
  39.2 3.0 %convert_element_type.35 = bf16[16,64,8,64]{3,2,1,0:T(8,128)(2,1)S(1)} reshape(bf16[1024,1,512]{2,0,1:T(8,128)(2,1)} %fusion.19) | data formatting | bytes 2097152 | tf_op jit(solution)/shard_map/convert_element_type | solution.py:33
  42.2 0.0 collective-permute-done
  42.2 1.7 constant_dynamic-update-slice_fusion.3
  43.9 0.0 collective-permute-done.1
  43.9 1.7 constant_dynamic-update-slice_fusion.2
  45.6 0.0 collective-permute-done.2
  45.6 1.7 constant_dynamic-update-slice_fusion.1
  47.2 0.3 collective-permute-done.3
  47.5 0.7 constant_dynamic-update-slice_fusion
  48.2 10.1 %gather_fusion = bf16[128,64,2,512]{3,1,2,0:T(8,128)(2,1)} fusion(bf16[24,64,2,512]{3,1,0,2:T(8,128)(2,1)} %constant_dynamic-update-slice_fusion, s32[1024]{0:T(1024)S(1)} %pad_clamp_fusion), kind=kCustom, calls=%fused_computation | custom fusion | bytes 33554944 | tf_op jit(solution)/shard_map/gather | solution.py:95
  58.3 14.1 %copy.13 = bf16[128,64,2,512]{3,1,0,2:T(8,128)(2,1)} copy(bf16[128,64,2,512]{3,1,2,0:T(8,128)(2,1)} %gather_fusion) | data formatting | bytes 33554432 | tf_op jit(solution)/shard_map/gather | solution.py:95
  72.5 66.3 %all-reduce.3.cloned.1.call-done = bf16[64,2,512]{2,0,1:T(8,128)(2,1)} async-done(((bf16[64,2,512]{2,0,1:T(8,128)(2,1)}), bf16[64,2,512]{2,0,1:T(8,128)(2,1)}) %all-reduce.3.cloned.1.call-update) | async-done | bytes 131088 | tf_op jit(solution)/shard_map/psum | solution.py:13
  138.8 2.5 broadcast_in_dim.41
  141.3 21.4 %pad_maximum_fusion = bf16[16,640,2,512]{3,1,0,2:T(8,128)(2,1)} fusion(bf16[16,64,2,512]{3,1,0,2:T(8,128)(2,1)} %broadcast_in_dim.41, bf16[16,512,2,512]{3,1,0,2:T(8,128)(2,1)} %bitcast.35, bf16[16,64,1,512]{3,1,0,2:T(8,128)(2,1)} %bitcast.40, bf16[16,64,1,512]{3,1,0,2:T(8,128)(2,1)} %bitcast.38), kind=kLoop, calls=%fused_computation.1 | loop fusion | flops 83886080 | bytes 41943040 | tf_op jit(solution)/shard_map/concatenate | solution.py:97
  162.6 16.1 %fusion.29 = (bf16[16,640,1,512]{3,1,0,2:T(8,128)(2,1)}, bf16[16,640,1,512]{3,1,0,2:T(8,128)(2,1)}) fusion(bf16[16,640,2,512]{3,1,0,2:T(8,128)(2,1)} %pad_maximum_fusion), kind=kLoop, calls=%fused_computation.54 | loop fusion | bytes 41943040 | tf_op jit(solution)/shard_map/slice | solution.py:42
  178.8 15.0 %copy.15 = bf16[16,640,1,512]{1,3,0,2:T(8,128)(2,1)} copy(bf16[16,640,1,512]{3,1,0,2:T(8,128)(2,1)} %get-tuple-element.5) | data formatting | bytes 20971520 | tf_op jit(solution)/shard_map/slice | solution.py:42
  193.8 14.5 %copy.14 = bf16[16,640,1,512]{1,3,0,2:T(8,128)(2,1)} copy(bf16[16,640,1,512]{3,1,0,2:T(8,128)(2,1)} %get-tuple-element.6) | data formatting | bytes 20971520 | tf_op jit(solution)/shard_map/slice | solution.py:43
  208.3 13.9 %select_reduce_fusion = (f32[16,8,64]{2,1,0:T(8,128)S(1)}, f32[16,8,64,640]{3,2,1,0:T(8,128)}) fusion(pred[16,640]{1,0:T(8,128)(4,1)S(1)} %pad_add_fusion, bf16[16,640,8,64]{1,3,2,0:T(8,128)(2,1)} %bitcast.34, bf16[16,64,8,64]{3,2,1,0:T(8,128)(2,1)S(1)} %convert_element_type.35), kind=kOutput, calls=%fused_computation.3 | convolution fusion | flops 681566208 | bytes 32548864 | tf_op jit(solution)/shard_map/pqhd,pkhd->phqk/dot_general | solution.py:44
  222.2 9.4 %fusion = f32[16,8,64]{2,1,0:T(8,128)S(1)} fusion(f32[16,8,64,640]{3,2,1,0:T(8,128)} %get-tuple-element.14, f32[16,8,64]{2,1,0:T(8,128)S(1)} %get-tuple-element.13, pred[16,640]{1,0:T(8,128)(4,1)S(1)} %pad_add_fusion), kind=kLoop, calls=%fused_computation.4 | loop fusion | flops 15720448 | bytes 21047296 | tf_op jit(solution)/shard_map/reduce_sum | solution.py:48
  231.7 13.5 %fusion.12 = bf16[16,64,8,64]{1,3,2,0:T(8,128)(2,1)} fusion(bf16[16,640,8,64]{1,3,2,0:T(8,128)(2,1)} %bitcast.36, f32[16,8,64,640]{3,2,1,0:T(8,128)} %get-tuple-element.14, f32[16,8,64]{2,1,0:T(8,128)S(1)} %get-tuple-element.13, pred[16,640]{1,0:T(8,128)(4,1)S(1)} %pad_add_fusion, f32[16,64,8]{1,2,0:T(8,128)S(1)} %bitcast.41), kind=kOutput, calls=%fused_computation.18 | convolution fusion | flops 687865856 | bytes 32581632 | tf_op jit(solution)/shard_map/phqk,pkhd->pqhd/dot_general | solution.py:50
  245.2 3.2 %copy.17 = bf16[16,64,8,64]{3,2,1,0:T(8,128)(2,1)S(1)} copy(bf16[16,64,8,64]{1,3,2,0:T(8,128)(2,1)} %fusion.12) | data formatting | bytes 2097152 | tf_op jit(solution)/shard_map/convert_element_type | solution.py:52
  248.4 2.0 reshape.46
  250.5 4.4 %fusion.33 = f32[1024,1024]{1,0:T(8,128)} fusion(bf16[1024,512]{1,0:T(8,128)(2,1)} %reshape.46, bf16[512,1024]{1,0:T(8,128)(2,1)S(1)} %copy-done), kind=kOutput, calls=%fused_computation.58 | convolution fusion | flops 1073741824 | bytes 6291456 | tf_op jit(solution)/shard_map/dot_general | solution.py:103
  254.9 17.7 %all-reduce.4 = bf16[1024,1024]{1,0:T(8,128)(2,1)} all-reduce(f32[1024,1024]{1,0:T(8,128)} %fusion.33), channel_id=1, replica_groups=mesh['region'=16,'mp'=2] {'mp'}, use_global_device_ids=true, to_apply=%region_5.6 | all-reduce | flops 1048576 | bytes 6291456 | tf_op jit(solution)/shard_map/psum | solution.py:104
  (17 shorter events, 0.1 us)
Async XLA Ops:
  6.5 244.0 %copy-start = (bf16[512,1024]{1,0:T(8,128)(2,1)S(1)}, bf16[512,1024]{1,0:T(8,128)(2,1)}, u32[]{:S(2)}) copy-start(bf16[512,1024]{1,0:T(8,128)(2,1)} %param.9) | copy-start | bytes 3145732
  6.5 132.3 %all-reduce.3.cloned.1.call-start = ((), (), s32[]{:S(2)}) async-start(), calls=%async_computation | async-start | bytes 262144 | tf_op jit(solution)/shard_map/psum | solution.py:13
  9.3 7.1 %copy-start.3 = (bf16[1024,1024]{1,0:T(8,128)(2,1)S(1)}, bf16[1024,1024]{1,0:T(8,128)(2,1)}, u32[]{:S(2)}) copy-start(bf16[1024,1024]{1,0:T(8,128)(2,1)} %param.6) | copy-start | bytes 6291460
  23.9 1.7 copy-start.4
  23.9 9.7 %copy-start.6 = (s32[16]{0:T(128)S(1)}, s32[16]{0:T(128)}, u32[]{:S(2)}) copy-start(s32[16]{0:T(128)} %param.11) | copy-start | bytes 196
  23.9 9.8 %copy-start.5 = (s32[16,8]{0,1:T(8,128)S(1)}, s32[16,8]{0,1:T(8,128)}, u32[]{:S(2)}) copy-start(s32[16,8]{0,1:T(8,128)} %param.10) | copy-start | bytes 1540
  26.5 17.4 %collective-permute-start.1 = (bf16[2,64,2,512]{3,1,0,2:T(8,128)(2,1)}, bf16[2,64,2,512]{3,1,0,2:T(8,128)(2,1)}, u32[]{:S(2)}, u32[]{:S(2)}) collective-permute-start(bf16[2,64,2,512]{3,1,0,2:T(8,128)(2,1)} %bitcast.6), channel_id=1, source_target_pairs={{28,0},{30,2},{0,4},{2,6},{4,8},{6,10},{8,12},{10,14},{12,16},{14,... | collective-permute-start | bytes 786440 | tf_op jit(solution)/shard_map/ppermute | solution.py:19
  27.7 14.4 %collective-permute-start = (bf16[2,64,2,512]{3,1,0,2:T(8,128)(2,1)}, bf16[2,64,2,512]{3,1,0,2:T(8,128)(2,1)}, u32[]{:S(2)}, u32[]{:S(2)}) collective-permute-start(bf16[2,64,2,512]{3,1,0,2:T(8,128)(2,1)} %bitcast.6), channel_id=1, source_target_pairs={{30,0},{0,2},{2,4},{4,6},{6,8},{8,10},{10,12},{12,14},{14,16},{16,... | collective-permute-start | bytes 786440 | tf_op jit(solution)/shard_map/ppermute | solution.py:19
  28.9 18.6 %collective-permute-start.3 = (bf16[2,64,2,512]{3,1,0,2:T(8,128)(2,1)}, bf16[2,64,2,512]{3,1,0,2:T(8,128)(2,1)S(1)}, u32[]{:S(2)}, u32[]{:S(2)}) collective-permute-start(bf16[2,64,2,512]{3,1,0,2:T(8,128)(2,1)} %bitcast.7), channel_id=1, source_target_pairs={{4,0},{6,2},{8,4},{10,6},{12,8},{14,10},{16,12},{18,14},{20,16},{2... | collective-permute-start | bytes 786440 | tf_op jit(solution)/shard_map/ppermute | solution.py:19
  30.1 15.5 %collective-permute-start.2 = (bf16[2,64,2,512]{3,1,0,2:T(8,128)(2,1)}, bf16[2,64,2,512]{3,1,0,2:T(8,128)(2,1)}, u32[]{:S(2)}, u32[]{:S(2)}) collective-permute-start(bf16[2,64,2,512]{3,1,0,2:T(8,128)(2,1)} %bitcast.7), channel_id=1, source_target_pairs={{2,0},{4,2},{6,4},{8,6},{10,8},{12,10},{14,12},{16,14},{18,16},{20... | collective-permute-start | bytes 786440 | tf_op jit(solution)/shard_map/ppermute | solution.py:19
  33.6 3.6 %copy-start.1 = (bf16[1024,1,512]{2,0,1:T(8,128)(2,1)}, bf16[1024,1,512]{2,0,1:T(8,128)(2,1)S(1)}, u32[]{:S(2)}) copy-start(bf16[1024,1,512]{2,0,1:T(8,128)(2,1)S(1)} %get-tuple-element.9) | copy-start | bytes 3145732
  33.6 5.1 %copy-start.2 = (bf16[1024,1,512]{2,0,1:T(8,128)(2,1)}, bf16[1024,1,512]{2,0,1:T(8,128)(2,1)S(1)}, u32[]{:S(2)}) copy-start(bf16[1024,1,512]{2,0,1:T(8,128)(2,1)S(1)} %get-tuple-element.10) | copy-start | bytes 3145732
Sparse Core Ops, SparseCore 0:
  32.0 106.7 all-reduce.2
where the time goes:
time: 283 us; the launch traced here: 279 us
  local copies, waits for them, and re-layouts  95.7 us (34%)
  waiting for transfers between devices  66.6 us (24%)
  other arithmetic  42.7 us (15%)
  matrix products  39.4 us (14%)
  blocking collectives  17.7 us (6%)
  between operations  13.5 us (5%)
  starting transfers between devices  3.83 us (1%)
    psum x1, waiting for transfers between devices, spread_2(): return lax.psum(kept, axis)  66.3 us
    slice x2, local copies, waits for them, and re-layouts, attend_block(): key_part = pairs[:, :, 0, :].reshape(npat, keys, heads, HDIM)  31.2 us
    gather x2, local copies, waits for them, and re-layouts, per_device(): far = table[slot].reshape(npat, NBR * patch, 2, feat)  24.2 us
    concatenate x1, other arithmetic, per_device(): keyed = jnp.concatenate([kv_pat, far, anchors], axis=1)  21.4 us
    psum x1, blocking collectives, per_device(): return lax.psum(partial_sum, 'mp').astype(jnp.bfloat16)  17.7 us
    slice x1, local copies, waits for them, and re-layouts, attend_block(): value_part = pairs[:, :, 1, :].reshape(npat, keys, heads, HDIM)  14.5 us
    dot_general x1, matrix products, attend_block(): jnp.einsum('pqhd,pkhd->phqk', query, key_part, preferred_element_type=jnp...  13.9 us
    dot_general x1, matrix products, attend_block(): jnp.einsum('phqk,pkhd->pqhd', weights, value_part, preferred_element_type...  13.5 us
  transfers between devices with their start and end apart: 5, of which 2 were waited for; matrix products, arithmetic and copies ran while one was open for 15% of the time, Pallas kernels for 0%

commit v1 on v0

v1 whole, which is shorter than its diff:
```python
import functools
import math

import jax
import jax.numpy as jnp
from jax import lax
from jax.experimental import pallas as pl
from jax.experimental.pallas import tpu as pltpu
from jax.sharding import PartitionSpec as P

HDIM = 64
NBR = 8
RIM = 2
GROUP = 4
MESH = pl.DeviceIdType.MESH


def kernel(
    n,
    tok_hbm,
    gain_ref,
    wqkv_hbm,
    wout_hbm,
    nbr_ref,
    deg_ref,
    out_hbm,
    tok,
    wqkv,
    wout,
    far_raw,
    anc_raw,
    q_tab,
    k_tab,
    v_tab,
    ctx,
    out,
    load_sem,
    anc_sem,
    anc_send,
    anc_recv,
    pair_send,
    pair_recv,
    far_send,
    far_recv,
    fwd_send,
    fwd_recv,
    ctx_send,
    ctx_recv,
    out_sem,
):
    rows, width = tok.shape
    patch = far_raw.shape[1]
    npat = rows // patch
    feat = q_tab.shape[1]
    half = patch // 2
    levels = max(1, math.ceil(math.log2(n)))
    far_n = 4 * RIM
    anchor_slot = npat + far_n
    region = lax.axis_index("region")
    core = lax.axis_index("mp")
    other = 1 - core

    chunk = 2 * patch
    nchunk = rows // chunk
    loads = [pltpu.make_async_copy(tok_hbm, tok, load_sem.at[0])]
    for j in range(3):
        loads.append(pltpu.make_async_copy(wqkv_hbm.at[j], wqkv.at[j], load_sem.at[1 + j]))
    loads.append(pltpu.make_async_copy(wout_hbm, wout.at[core], load_sem.at[4]))
    for c in loads:
        c.start()

    ring = [lax.rem(region + d + n, n) for d in (1, 2, -1, -2)]
    has_child, has_parent = [], []
    for j in range(levels):
        step, span = 2**j, 2 ** (j + 1)
        has_child.append(jnp.logical_and(lax.rem(region, span) == 0, region + step < n))
        has_parent.append(lax.rem(region, span) == step)

    depth = jnp.int32(0)
    for j in range(levels):
        depth = depth + lax.rem(region // (2**j), 2)

    barrier = pltpu.get_barrier_semaphore()
    for target in ring:
        pl.semaphore_signal(barrier, inc=1, device_id=(target, core), device_id_type=MESH)
    pl.semaphore_signal(barrier, inc=1, device_id=(region, other), device_id_type=MESH)
    links = jnp.int32(5)
    for j in range(levels):
        links = links + has_child[j].astype(jnp.int32) + has_parent[j].astype(jnp.int32)

        @pl.when(has_child[j])
        def _():
            pl.semaphore_signal(barrier, inc=1, device_id=(region + 2**j, core), device_id_type=MESH)

        @pl.when(has_parent[j])
        def _():
            pl.semaphore_signal(barrier, inc=1, device_id=(region - 2**j, core), device_id_type=MESH)

    pl.semaphore_wait(barrier, links)

    def anc_copy(j):
        return pltpu.make_async_remote_copy(
            src_ref=anc_raw.at[core],
            dst_ref=anc_raw.at[core],
            send_sem=anc_send.at[j],
            recv_sem=anc_recv,
            device_id=(lax.rem(region + 2**j, n), core),
            device_id_type=MESH,
        )

    def pair_copy(which):
        return pltpu.make_async_remote_copy(
            src_ref=anc_raw.at[which],
            dst_ref=anc_raw.at[which],
            send_sem=pair_send.at[0],
            recv_sem=pair_recv.at[0],
            device_id=(region, other),
            device_id_type=MESH,
        )

    def wout_copy(which):
        return pltpu.make_async_remote_copy(
            src_ref=wout_hbm,
            dst_ref=wout.at[which],
            send_sem=pair_send.at[1],
            recv_sem=pair_recv.at[1],
            device_id=(region, other),
            device_id_type=MESH,
        )

    def far_copy(d):
        first = (npat - RIM if d < 2 else 0) + core
        return pltpu.make_async_remote_copy(
            src_ref=tok_hbm.at[pl.ds(pl.multiple_of(first * patch, patch), patch)],
            dst_ref=far_raw.at[d * RIM + core],
            send_sem=far_send.at[d],
            recv_sem=far_recv.at[d],
            device_id=(ring[d], core),
            device_id_type=MESH,
        )

    def fwd_copy(d, which):
        return pltpu.make_async_remote_copy(
            src_ref=far_raw.at[d * RIM + which],
            dst_ref=far_raw.at[d * RIM + which],
            send_sem=fwd_send.at[d],
            recv_sem=fwd_recv.at[d],
            device_id=(region, other),
            device_id_type=MESH,
        )

    size = GROUP * patch

    def ctx_copy(g, which):
        span = pl.ds(pl.multiple_of(g * size, size), size)
        return pltpu.make_async_remote_copy(
            src_ref=ctx.at[which, span],
            dst_ref=ctx.at[which, span],
            send_sem=ctx_send.at[g],
            recv_sem=ctx_recv.at[g],
            device_id=(region, other),
            device_id_type=MESH,
        )

    def pass_anchor():
        @pl.when(region == 0)
        def _():
            mine = pltpu.make_async_copy(
                tok_hbm.at[pl.ds(pl.multiple_of(core * half, half), half)], anc_raw.at[core], anc_sem
            )
            mine.start()
            mine.wait()

        @pl.when(region > 0)
        def _():
            anc_copy(0).wait_recv()

        for j in reversed(range(levels)):

            @pl.when(has_child[j])
            def _():
                anc_copy(j).start()

        pair_copy(core).start()
        for d in range(4):
            far_copy(d).start()

    wout_copy(core).start()

    gain = gain_ref[...].astype(jnp.float32)

    def normalise(raw):
        values = raw.astype(jnp.float32)
        centre = jnp.mean(values, axis=-1, keepdims=True)
        away = values - centre
        spread = jnp.mean(away * away, axis=-1, keepdims=True)
        return (away * lax.rsqrt(spread + 1e-05) * gain).astype(jnp.bfloat16)

    def key_value(normed, first, count):
        for tab, j in ((k_tab, 1), (v_tab, 2)):
            part = jnp.dot(normed, wqkv[j], preferred_element_type=jnp.float32)
            tab[pl.ds(first, count)] = part.astype(jnp.bfloat16).reshape(count, patch, feat)

    for c in loads:
        c.wait()

    def qkv_step(i, carry):
        span = pl.ds(pl.multiple_of(i * chunk, chunk), chunk)
        normed = normalise(tok[span])
        part = jnp.dot(normed, wqkv[0], preferred_element_type=jnp.float32)
        q_tab[span] = (part * (1.0 / HDIM**0.5)).astype(jnp.bfloat16)
        key_value(normed, i * 2, 2)

        @pl.when(i == jnp.minimum(depth * 2, nchunk - 1))
        def _():
            pass_anchor()

        return carry

    lax.fori_loop(0, nchunk, qkv_step, 0)

    pair_copy(other).wait_recv()
    key_value(normalise(anc_raw[...].reshape(patch, width)), anchor_slot, 1)

    block = GROUP * HDIM
    keys = (NBR + 2) * patch
    lane = lax.broadcasted_iota(jnp.int32, (patch, block), 1) // HDIM
    column = lax.broadcasted_iota(jnp.int32, (1, keys), 1)

    def attend(t):
        p = lax.rem(t + RIM, npat)
        deg = deg_ref[p]
        slots = [p]
        for j in range(NBR):
            nb = nbr_ref[j, p]
            owner, local = nb // npat, lax.rem(nb, npat)
            reach = lax.rem(owner - region + n, n)
            slot = jnp.where(
                reach == 0,
                local,
                jnp.where(
                    reach == n - 1,
                    local + RIM,
                    jnp.where(
                        reach == n - 2,
                        local + 2 * RIM,
                        jnp.where(reach == 1, npat + 2 * RIM + local, npat + 3 * RIM + local),
                    ),
                ),
            )
            slots.append(jnp.where(j < deg, slot, p))
        slots.append(anchor_slot)
        valid = jnp.logical_or(column < (deg + 1) * patch, column >= (NBR + 1) * patch)
        at = pl.ds(pl.multiple_of(p * patch, patch), patch)
        to = pl.ds(pl.multiple_of(t * patch, patch), patch)
        for b in range(feat // block):
            cols = slice(b * block, (b + 1) * block)
            qb = q_tab[at, cols]
            zero = jnp.zeros_like(qb)
            spread = jnp.concatenate([jnp.where(lane == i, qb, zero) for i in range(GROUP)], axis=0)
            kk = jnp.concatenate([k_tab[s, :, cols] for s in slots], axis=0)
            vv = jnp.concatenate([v_tab[s, :, cols] for s in slots], axis=0)
            scores = lax.dot_general(
                spread, kk, (((1,), (1,)), ((), ())), preferred_element_type=jnp.float32
            )
            scores = jnp.where(valid, scores, jnp.float32(-1e30))
            top = jnp.max(scores, axis=-1, keepdims=True)
            expo = jnp.exp(scores - top)
            total = jnp.sum(expo, axis=-1, keepdims=True)
            mixed = jnp.dot(expo.astype(jnp.bfloat16), vv, preferred_element_type=jnp.float32) / total
            packed = jnp.where(lane == 0, mixed[:patch], 0.0)
            for i in range(1, GROUP):
                packed = jnp.where(lane == i, mixed[i * patch : (i + 1) * patch], packed)
            ctx[core, to, cols] = packed.astype(jnp.bfloat16)

    rim_rows = RIM * patch

    def project(g):
        span = pl.ds(pl.multiple_of(g * size, size), size)
        ctx_copy(g, other).wait_recv()
        total = jnp.dot(ctx[0, span], wout[0], preferred_element_type=jnp.float32)
        total = total + jnp.dot(ctx[1, span], wout[1], preferred_element_type=jnp.float32)
        out[span] = total.astype(jnp.bfloat16)

    def inner_out(g):
        return pltpu.make_async_copy(
            out.at[pl.ds(pl.multiple_of(g * size, size), size)],
            out_hbm.at[pl.ds(pl.multiple_of(g * size + rim_rows, rim_rows), size)],
            out_sem.at[g],
        )

    ngroup = npat // GROUP

    def group_step(g, carry):
        @pl.when(g == 1)
        def _():
            for d in range(4):
                far_copy(d).wait_recv()
                fwd_copy(d, core).start()
            wout_copy(other).wait_recv()

        @pl.when(g == ngroup - 1)
        def _():
            for d in range(4):
                fwd_copy(d, other).wait_recv()

            def far_step(d, c):
                raw = far_raw[pl.ds(d * RIM, RIM)].reshape(rim_rows, width)
                key_value(normalise(raw), npat + d * RIM, RIM)
                return c

            lax.fori_loop(0, 4, far_step, 0)

        def patch_step(u, c):
            attend(g * GROUP + u)
            return c

        lax.fori_loop(0, GROUP, patch_step, 0)
        ctx_copy(g, core).start()

        @pl.when(g >= 1)
        def _():
            project(g - 1)
            inner_out(g - 1).start()

        return carry

    lax.fori_loop(0, ngroup, group_step, 0)
    project(ngroup - 1)
    tail = rows - size
    last = [
        pltpu.make_async_copy(
            out.at[pl.ds(tail, rim_rows)], out_hbm.at[pl.ds(rows - rim_rows, rim_rows)], out_sem.at[ngroup - 1]
        ),
        pltpu.make_async_copy(
            out.at[pl.ds(tail + rim_rows, rim_rows)], out_hbm.at[pl.ds(0, rim_rows)], out_sem.at[ngroup]
        ),
    ]
    for c in last:
        c.start()

    for j in range(levels):

        @pl.when(has_child[j])
        def _():
            anc_copy(j).wait_send()

    pair_copy(core).wait_send()
    wout_copy(core).wait_send()
    for d in range(4):
        far_copy(d).wait_send()
        fwd_copy(d, core).wait_send()
    for g in range(ngroup):
        ctx_copy(g, core).wait_send()
    for g in range(ngroup - 1):
        inner_out(g).wait()
    for c in last:
        c.wait()


def solution(mesh):
    n = mesh.shape["region"]

    def per_device(tokens, ln_gain, w_qkv, w_out, neighbours, degree):
        rows, width = tokens.shape
        npat = neighbours.shape[0]
        patch = rows // npat
        feat = w_qkv.shape[2]
        levels = max(1, math.ceil(math.log2(n)))
        ngroup = npat // GROUP
        slots = npat + 4 * RIM + 1
        any_spec = pl.BlockSpec(memory_space=pl.ANY)
        smem = pl.BlockSpec(memory_space=pltpu.SMEM)
        dma = pltpu.SemaphoreType.DMA
        bf = jnp.bfloat16
        return pl.pallas_call(
            functools.partial(kernel, n),
            out_shape=jax.ShapeDtypeStruct((rows, width), bf),
            in_specs=[
                any_spec,
                pl.BlockSpec(memory_space=pltpu.VMEM),
                any_spec,
                any_spec,
                smem,
                smem,
            ],
            out_specs=any_spec,
            scratch_shapes=[
                pltpu.VMEM((rows, width), bf),
                pltpu.VMEM((3, width, feat), bf),
                pltpu.VMEM((2, feat, width), bf),
                pltpu.VMEM((4 * RIM, patch, width), bf),
                pltpu.VMEM((2, patch // 2, width), bf),
                pltpu.VMEM((rows, feat), bf),
                pltpu.VMEM((slots, patch, feat), bf),
                pltpu.VMEM((slots, patch, feat), bf),
                pltpu.VMEM((2, rows, feat), bf),
                pltpu.VMEM((rows, width), bf),
                dma((5,)),
                dma,
                dma((levels,)),
                dma,
                dma((2,)),
                dma((2,)),
                dma((4,)),
                dma((4,)),
                dma((4,)),
                dma((4,)),
                dma((ngroup,)),
                dma((ngroup,)),
                dma((ngroup + 1,)),
            ],
            compiler_params=pltpu.CompilerParams(
                collective_id=0, has_side_effects=True, vmem_limit_bytes=56 * 2**20
            ),
            name="patch_attention",
        )(
            tokens,
            ln_gain.reshape(1, width),
            jnp.transpose(w_qkv, (1, 0, 2)),
            w_out,
            jnp.transpose(neighbours),
            degree,
        )

    placed = (
        P("region", None),
        P(),
        P(None, None, "mp"),
        P("mp", None),
        P("region", None),
        P("region"),
    )
    return jax.shard_map(
        per_device, mesh=mesh, in_specs=placed, out_specs=P("region", None), check_vma=False
    )
```

time: 283 us -> 56.5 us (0.20)
  the two profiles are of different devices: /device:TPU:11 before, /device:TPU:1 now
where the time goes in v1:
time: 56.5 us; the launch traced here: 56.2 us
  Pallas kernels  51.8 us (92%)
  local copies, waits for them, and re-layouts  4.36 us (8%)
    pallas_call x1, Pallas kernels, per_device(): pl.pallas_call(functools.partial(kernel, n), out_shape=jax.ShapeDtypeStru...  51.8 us
    unnamed x1, local copies, waits for them, and re-layouts  3.08 us
    reshape x1, local copies, waits for them, and re-layouts, per_device(): ln_gain.reshape(1, width)  1.28 us

profile of v1, /device:TPU:1, one launch (start us, length us, event | category | flops | bytes accessed | tf_op | source)
XLA Modules:
  0.0 56.2 jit_solution(5021749676591230997)
XLA Ops:
  0.0 1.3 %reshape.3.gain_ref = bf16[1,1024]{1,0:T(2,128)(2,1)} reshape(bf16[1024]{0:T(1024)(128)(2,1)} %param.7) | data formatting | bytes 4096 | tf_op jit(solution)/shard_map/reshape | solution.py:419
  1.3 51.8 %patch_attention.1 = bf16[1024,1024]{1,0:T(8,128)(2,1)} custom-call(bf16[1024,1024]{1,0:T(8,128)(2,1)} %tok_hbm.1, bf16[1,1024]{1,0:T(2,128)(2,1)} %reshape.3.gain_ref, bf16[3,1024,512]{2,1,0:T(8,128)(2,1)} %bitcast.2, bf16[512,1024]{1,0:T(8,128)(2,1)} %wout_hbm.1, s32[8,16]{1,0:T(8,128)} %bitcast.3, s32[16]{0:T(128)} %deg_ref.1), custom_call_target="tpu_custom_call" | custom-call | tf_op jit(solution)/shard_map/patch_attention/pallas_call | solution.py:376
  53.1 3.1 %copy.8 = bf16[1024,1024]{1,0:T(8,128)(2,1)} copy(bf16[1024,1024]{1,0:T(8,128)(2,1)} %patch_attention.1) | data formatting | bytes 4194304

commit v2 on v1

--- a/solution.py
+++ b/solution.py
@@ -1,5 +1,4 @@
 import functools
-import math
 
 import jax
 import jax.numpy as jnp
@@ -12,7 +11,16 @@
 NBR = 8
 RIM = 2
 GROUP = 4
+FAN = 4
+EARLY = 2
 MESH = pl.DeviceIdType.MESH
+
+
+def tree_levels(n):
+    levels = 1
+    while FAN**levels < n:
+        levels += 1
+    return levels
 
 
 def kernel(
@@ -53,7 +61,7 @@
     npat = rows // patch
     feat = q_tab.shape[1]
     half = patch // 2
-    levels = max(1, math.ceil(math.log2(n)))
+    levels = tree_levels(n)
     far_n = 4 * RIM
     anchor_slot = npat + far_n
     region = lax.axis_index("region")
@@ -70,33 +78,30 @@
         c.start()
 
     ring = [lax.rem(region + d + n, n) for d in (1, 2, -1, -2)]
-    has_child, has_parent = [], []
-    for j in range(levels):
-        step, span = 2**j, 2 ** (j + 1)
-        has_child.append(jnp.logical_and(lax.rem(region, span) == 0, region + step < n))
-        has_parent.append(lax.rem(region, span) == step)
-
+    children, parents = [], []
     depth = jnp.int32(0)
-    for j in range(levels):
-        depth = depth + lax.rem(region // (2**j), 2)
+    for level in range(levels):
+        step = FAN**level
+        digit = lax.rem(region // step, FAN)
+        depth = depth + (digit > 0).astype(jnp.int32)
+        alone = lax.rem(region, step) == 0
+        for j in range(1, FAN):
+            target = region + j * step
+            children.append((jnp.logical_and(lax.rem(region, step * FAN) == 0, target < n), target))
+            parents.append((jnp.logical_and(alone, digit == j), region - j * step))
+    near = region < EARLY
 
     barrier = pltpu.get_barrier_semaphore()
     for target in ring:
         pl.semaphore_signal(barrier, inc=1, device_id=(target, core), device_id_type=MESH)
     pl.semaphore_signal(barrier, inc=1, device_id=(region, other), device_id_type=MESH)
     links = jnp.int32(5)
-    for j in range(levels):
-        links = links + has_child[j].astype(jnp.int32) + has_parent[j].astype(jnp.int32)
-
-        @pl.when(has_child[j])
-        def _():
-            pl.semaphore_signal(barrier, inc=1, device_id=(region + 2**j, core), device_id_type=MESH)
-
-        @pl.when(has_parent[j])
-        def _():
-            pl.semaphore_signal(barrier, inc=1, device_id=(region - 2**j, core), device_id_type=MESH)
-
-    pl.semaphore_wait(barrier, links)
+    for there, target in children + parents:
+        links = links + there.astype(jnp.int32)
+
+        @pl.when(there)
+        def _():
+            pl.semaphore_signal(barrier, inc=1, device_id=(target, core), device_id_type=MESH)
 
     def anc_copy(j):
         return pltpu.make_async_remote_copy(
@@ -104,7 +109,7 @@
             dst_ref=anc_raw.at[core],
             send_sem=anc_send.at[j],
             recv_sem=anc_recv,
-            device_id=(lax.rem(region + 2**j, n), core),
+            device_id=(lax.rem(children[j][1], n), core),
             device_id_type=MESH,
         )
 
@@ -162,7 +167,22 @@
             device_id_type=MESH,
         )
 
-    def pass_anchor():
+    def send_anchor():
+        for j in reversed(range(len(children))):
+
+            @pl.when(children[j][0])
+            def _():
+                anc_copy(j).start()
+
+        pair_copy(core).start()
+
+    def send_far():
+        for d in range(4):
+            far_copy(d).start()
+
+    def enter():
+        pl.semaphore_wait(barrier, links)
+
         @pl.when(region == 0)
         def _():
             mine = pltpu.make_async_copy(
@@ -170,22 +190,14 @@
             )
             mine.start()
             mine.wait()
-
-        @pl.when(region > 0)
-        def _():
-            anc_copy(0).wait_recv()
-
-        for j in reversed(range(levels)):
-
-            @pl.when(has_child[j])
-            def _():
-                anc_copy(j).start()
-
-        pair_copy(core).start()
-        for d in range(4):
-            far_copy(d).start()
-
-    wout_copy(core).start()
+            send_anchor()
+
+        send_far()
+        wout_copy(core).start()
+
+    def relay():
+        anc_copy(0).wait_recv()
+        send_anchor()
 
     gain = gain_ref[...].astype(jnp.float32)
 
@@ -201,19 +213,28 @@
             part = jnp.dot(normed, wqkv[j], preferred_element_type=jnp.float32)
             tab[pl.ds(first, count)] = part.astype(jnp.bfloat16).reshape(count, patch, feat)
 
-    for c in loads:
-        c.wait()
+    enter_at = jnp.where(near, nchunk - 1, 0)
+    relay_at = jnp.where(near, nchunk - 1, jnp.minimum(3 * depth, nchunk - 1))
 
     def qkv_step(i, carry):
+        @pl.when(i == enter_at)
+        def _():
+            enter()
+
+        @pl.when(i == 0)
+        def _():
+            for c in loads:
+                c.wait()
+
         span = pl.ds(pl.multiple_of(i * chunk, chunk), chunk)
         normed = normalise(tok[span])
         part = jnp.dot(normed, wqkv[0], preferred_element_type=jnp.float32)
         q_tab[span] = (part * (1.0 / HDIM**0.5)).astype(jnp.bfloat16)
         key_value(normed, i * 2, 2)
 
-        @pl.when(i == jnp.minimum(depth * 2, nchunk - 1))
-        def _():
-            pass_anchor()
+        @pl.when(jnp.logical_and(i == relay_at, region > 0))
+        def _():
+            relay()
 
         return carry
 
@@ -291,24 +312,26 @@
 
     ngroup = npat // GROUP
 
+    def swap_far():
+        for d in range(4):
+            far_copy(d).wait_recv()
+            fwd_copy(d, core).start()
+        wout_copy(other).wait_recv()
+
+    def far_step(d, c):
+        raw = far_raw[pl.ds(d * RIM, RIM)].reshape(rim_rows, width)
+        key_value(normalise(raw), npat + d * RIM, RIM)
+        return c
+
     def group_step(g, carry):
         @pl.when(g == 1)
         def _():
-            for d in range(4):
-                far_copy(d).wait_recv()
-                fwd_copy(d, core).start()
-            wout_copy(other).wait_recv()
+            swap_far()
 
         @pl.when(g == ngroup - 1)
         def _():
             for d in range(4):
                 fwd_copy(d, other).wait_recv()
-
-            def far_step(d, c):
-                raw = far_raw[pl.ds(d * RIM, RIM)].reshape(rim_rows, width)
-                key_value(normalise(raw), npat + d * RIM, RIM)
-                return c
-
             lax.fori_loop(0, 4, far_step, 0)
 
         def patch_step(u, c):
@@ -339,9 +362,9 @@
     for c in last:
         c.start()
 
-    for j in range(levels):
-
-        @pl.when(has_child[j])
+    for j in range(len(children)):
+
+        @pl.when(children[j][0])
         def _():
             anc_copy(j).wait_send()
 
@@ -366,25 +389,25 @@
         npat = neighbours.shape[0]
         patch = rows // npat
         feat = w_qkv.shape[2]
-        levels = max(1, math.ceil(math.log2(n)))
+        levels = tree_levels(n)
         ngroup = npat // GROUP
         slots = npat + 4 * RIM + 1
-        any_spec = pl.BlockSpec(memory_space=pl.ANY)
+        hbm = pl.BlockSpec(memory_space=pltpu.HBM)
         smem = pl.BlockSpec(memory_space=pltpu.SMEM)
         dma = pltpu.SemaphoreType.DMA
         bf = jnp.bfloat16
         return pl.pallas_call(
             functools.partial(kernel, n),
-            out_shape=jax.ShapeDtypeStruct((rows, width), bf),
+            out_shape=pltpu.VMEM((rows, width), bf),
             in_specs=[
-                any_spec,
+                hbm,
                 pl.BlockSpec(memory_space=pltpu.VMEM),
-                any_spec,
-                any_spec,
+                hbm,
+                hbm,
                 smem,
                 smem,
             ],
-            out_specs=any_spec,
+            out_specs=pl.BlockSpec(memory_space=pl.ANY),
             scratch_shapes=[
                 pltpu.VMEM((rows, width), bf),
                 pltpu.VMEM((3, width, feat), bf),
@@ -398,7 +421,7 @@
                 pltpu.VMEM((rows, width), bf),
                 dma((5,)),
                 dma,
-                dma((levels,)),
+                dma(((FAN - 1) * levels,)),
                 dma,
                 dma((2,)),
                 dma((2,)),
@@ -411,12 +434,12 @@
                 dma((ngroup + 1,)),
             ],
             compiler_params=pltpu.CompilerParams(
-                collective_id=0, has_side_effects=True, vmem_limit_bytes=56 * 2**20
+                collective_id=0, has_side_effects=True, vmem_limit_bytes=60 * 2**20
             ),
             name="patch_attention",
         )(
             tokens,
-            ln_gain.reshape(1, width),
+            ln_gain,
             jnp.transpose(w_qkv, (1, 0, 2)),
             w_out,
             jnp.transpose(neighbours),

time: 56.5 us -> 43.8 us (0.78)
  the two profiles are of different devices: /device:TPU:1 before, /device:TPU:11 now
where the time goes in v2:
time: 43.8 us; the launch traced here: 43.6 us
  Pallas kernels  42.3 us (97%)
  local copies, waits for them, and re-layouts  1.32 us (3%)
    pallas_call x1, Pallas kernels, per_device(): pl.pallas_call(functools.partial(kernel, n), out_shape=pltpu.VMEM((rows,...  42.3 us
    unnamed x1, local copies, waits for them, and re-layouts  1.32 us

profile of v2, /device:TPU:11, one launch (start us, length us, event | category | flops | bytes accessed | tf_op | source)
XLA Modules:
  0.0 43.6 jit_solution(18269834180262208763)
XLA Ops:
  0.0 42.3 %patch_attention.1 = bf16[1024,1024]{1,0:T(8,128)(2,1)S(1)} custom-call(bf16[1024,1024]{1,0:T(8,128)(2,1)} %tok_hbm.1, bf16[1024]{0:T(1024)(128)(2,1)} %gain_ref.1, bf16[3,1024,512]{2,1,0:T(8,128)(2,1)} %bitcast.2, bf16[512,1024]{1,0:T(8,128)(2,1)} %wout_hbm.1, s32[8,16]{1,0:T(8,128)} %bitcast.3, s32[16]{0:T(128)} %deg_ref.1), custom_call_target="tpu_custom_call" | custom-call | tf_op jit(solution)/shard_map/patch_attention/pallas_call | solution.py:399
  42.3 1.3 %copy.8 = bf16[1024,1024]{1,0:T(8,128)(2,1)} copy(bf16[1024,1024]{1,0:T(8,128)(2,1)S(1)} %patch_attention.1) | data formatting | bytes 4194304

commit v3 on v2

--- a/solution.py
+++ b/solution.py
@@ -68,7 +68,7 @@
     core = lax.axis_index("mp")
     other = 1 - core
 
-    chunk = 2 * patch
+    chunk = 8 * patch
     nchunk = rows // chunk
     loads = [pltpu.make_async_copy(tok_hbm, tok, load_sem.at[0])]
     for j in range(3):
@@ -214,7 +214,7 @@
             tab[pl.ds(first, count)] = part.astype(jnp.bfloat16).reshape(count, patch, feat)
 
     enter_at = jnp.where(near, nchunk - 1, 0)
-    relay_at = jnp.where(near, nchunk - 1, jnp.minimum(3 * depth, nchunk - 1))
+    relay_at = jnp.where(near, nchunk - 1, jnp.minimum(depth - 1, nchunk - 1))
 
     def qkv_step(i, carry):
         @pl.when(i == enter_at)
@@ -230,7 +230,7 @@
         normed = normalise(tok[span])
         part = jnp.dot(normed, wqkv[0], preferred_element_type=jnp.float32)
         q_tab[span] = (part * (1.0 / HDIM**0.5)).astype(jnp.bfloat16)
-        key_value(normed, i * 2, 2)
+        key_value(normed, i * 8, 8)
 
         @pl.when(jnp.logical_and(i == relay_at, region > 0))
         def _():
@@ -319,8 +319,8 @@
         wout_copy(other).wait_recv()
 
     def far_step(d, c):
-        raw = far_raw[pl.ds(d * RIM, RIM)].reshape(rim_rows, width)
-        key_value(normalise(raw), npat + d * RIM, RIM)
+        raw = far_raw[pl.ds(d * 2 * RIM, 2 * RIM)].reshape(2 * rim_rows, width)
+        key_value(normalise(raw), npat + d * 2 * RIM, 2 * RIM)
         return c
 
     def group_step(g, carry):
@@ -332,13 +332,13 @@
         def _():
             for d in range(4):
                 fwd_copy(d, other).wait_recv()
-            lax.fori_loop(0, 4, far_step, 0)
+            lax.fori_loop(0, 2, far_step, 0)
 
         def patch_step(u, c):
             attend(g * GROUP + u)
             return c
 
-        lax.fori_loop(0, GROUP, patch_step, 0)
+        lax.fori_loop(0, GROUP, patch_step, 0, unroll=4)
         ctx_copy(g, core).start()
 
         @pl.when(g >= 1)

time: 43.8 us -> 35.6 us (0.81)
  Pallas kernels: 42.3 us -> 33.9 us
    pallas_call x1, Pallas kernels: 42.3 us -> 33.9 us  [per_device(): pl.pallas_call(functools.partial(kernel, n), out_shape=pltpu.VMEM((rows,...]
where the time goes in v3:
time: 35.6 us; the launch traced here: 35.3 us
  Pallas kernels  33.9 us (95%)
  local copies, waits for them, and re-layouts  1.32 us (4%)
    pallas_call x1, Pallas kernels, per_device(): pl.pallas_call(functools.partial(kernel, n), out_shape=pltpu.VMEM((rows,...  33.9 us
    unnamed x1, local copies, waits for them, and re-layouts  1.32 us

profile of v3, /device:TPU:11, one launch (start us, length us, event | category | flops | bytes accessed | tf_op | source)
XLA Modules:
  0.0 35.3 jit_solution(14554591289554295490)
XLA Ops:
  0.0 33.9 %patch_attention.1 = bf16[1024,1024]{1,0:T(8,128)(2,1)S(1)} custom-call(bf16[1024,1024]{1,0:T(8,128)(2,1)} %tok_hbm.1, bf16[1024]{0:T(1024)(128)(2,1)} %gain_ref.1, bf16[3,1024,512]{2,1,0:T(8,128)(2,1)} %bitcast.2, bf16[512,1024]{1,0:T(8,128)(2,1)} %wout_hbm.1, s32[8,16]{1,0:T(8,128)} %bitcast.3, s32[16]{0:T(128)} %deg_ref.1), custom_call_target="tpu_custom_call" | custom-call | tf_op jit(solution)/shard_map/patch_attention/pallas_call | solution.py:399
  34.0 1.3 %copy.8 = bf16[1024,1024]{1,0:T(8,128)(2,1)} copy(bf16[1024,1024]{1,0:T(8,128)(2,1)S(1)} %patch_attention.1) | data formatting | bytes 4194304
